TPU v7x, 512 devices: a whole 4x8x8 slice. The times are simulated.
512 devices in a mesh: ctx: 64 (over x, z_lo, y), head: 8 (over z_hi, core).
Axes of the slice: x: 4, y: 8, z: 8 (z_hi: 4, z_lo: 2; z = z_hi * 2 + z_lo), core: 2. Of those that a mesh axis runs over, the one named last changes fastest.
Arguments:
- queries: bfloat16 [8192, 4096], P(('ctx', 'head')), may hold values from -30 to 30
- keys: bfloat16 [8192, 1024], P(('ctx', 'head')), may hold values from -6 to 6
- values: bfloat16 [8192, 1024], P(('ctx', 'head')), may hold values from -6 to 6
- outputs: bfloat16 [8192, 4096], P(('ctx', 'head')), may hold values from -6 to 6
- output_gradient: bfloat16 [8192, 4096], P(('ctx', 'head')), may hold values from -6 to 6
- importance: int32 [8192], P('ctx'), may hold values from 0 to 8
- span_order: int32 [128], replicated, may hold values from 0 to 127, each once
Outputs:
- query_grad: bfloat16 [8192, 4096], P(('ctx', 'head'))
- key_gradient: bfloat16 [8192, 1024], P(('ctx', 'head'))
- value_gradient: bfloat16 [8192, 1024], P(('ctx', 'head'))
All inputs are finite; a program needn't handle non-finite values.
Results may differ from a plain program's by a relative error of at most 0.0049.
Values may be sent and summed in bfloat16 or wider, within the bound.
A program may use at most 64 MiB of HBM per device.

v0:
```python
import math
import jax
import jax.numpy as jnp
from jax import lax
from jax.sharding import PartitionSpec as P

QUERY_HEADS = 32
KEY_VALUE_HEADS = 8
HEAD_WIDTH = 128
CH = 64
very_low = -1e30


def shifted(array, axis, by):
    size = lax.axis_size(axis)
    return lax.ppermute(array, axis, [(i, (i + by) % size) for i in range(size)])


def key_positions(span_order):
    span_count = span_order.shape[0]
    token_index = jnp.arange(span_count * CH, dtype=jnp.int32)
    span_index = token_index // CH
    matches = span_index[:, None] == jnp.arange(span_count, dtype=jnp.int32)[None, :]
    return jnp.sum(jnp.where(matches, span_order[None, :], 0), axis=1) * CH + token_index % CH


def block_split(length):
    if length > 512 and length % 512 == 0:
        return (512, length // 512)
    return (length, 1)


def on_device(queries, keys, values, outputs, output_gradient, importance, span_order):
    query_loc, output_loc, grad_loc, key_loc, value_loc = (
        lax.all_to_all(queries, "head", split_axis=1, concat_axis=0, tiled=True),
        lax.all_to_all(outputs, "head", split_axis=1, concat_axis=0, tiled=True),
        lax.all_to_all(output_gradient, "head", split_axis=1, concat_axis=0, tiled=True),
        lax.all_to_all(keys, "head", split_axis=1, concat_axis=0, tiled=True),
        lax.all_to_all(values, "head", split_axis=1, concat_axis=0, tiled=True),
    )
    row_count = query_loc.shape[0]
    kv_local = key_loc.shape[1] // HEAD_WIDTH
    group_width = QUERY_HEADS // KEY_VALUE_HEADS
    score_scale = 1.0 / math.sqrt(HEAD_WIDTH)
    cycle_count = lax.axis_size("ctx")
    my_index = lax.axis_index("ctx")
    heads_of_queries = query_loc.reshape(row_count, kv_local, group_width, HEAD_WIDTH)
    gradient_heads = grad_loc.reshape(row_count, kv_local, group_width, HEAD_WIDTH)
    output_heads = output_loc.reshape(row_count, kv_local, group_width, HEAD_WIDTH)
    out_dot = jnp.sum(
        gradient_heads.astype(jnp.float32) * output_heads.astype(jnp.float32), axis=-1
    )
    all_positions = key_positions(span_order)
    query_pos = lax.dynamic_slice_in_dim(all_positions, my_index * row_count, row_count)
    token_gain = importance.astype(jnp.float32) * 0.25
    grad_scale = (token_gain * score_scale)[:, None, None, None]
    gain_wide = token_gain[:, None, None, None]

    def scores_of(key_block, key_pos):
        key_split = key_block.reshape(key_block.shape[0], kv_local, HEAD_WIDTH)
        raw_scores = (
            jnp.einsum(
                "rcgd,ncd->rcgn", heads_of_queries, key_split, preferred_element_type=jnp.float32
            )
            * score_scale
        )
        visible = key_pos[None, None, None, :] <= query_pos[:, None, None, None]
        return (key_split, raw_scores, visible)

    def stats_block(running, inputs):
        key_split, raw_scores, visible = scores_of(inputs[0], inputs[1])
        masked = jnp.where(visible, raw_scores, very_low)
        running_max = jnp.maximum(running[0], jnp.max(masked, axis=-1))
        denominator = running[1] * jnp.exp(running[0] - running_max) + jnp.sum(
            jnp.where(visible, jnp.exp(masked - running_max[..., None]), 0.0), axis=-1
        )
        return ((running_max, denominator), None)

    def grads_block(log_norm, key_block, value_block, key_pos):
        key_split, raw_scores, visible = scores_of(key_block, key_pos)
        value_split = value_block.reshape(value_block.shape[0], kv_local, HEAD_WIDTH)
        probs = jnp.where(visible, jnp.exp(raw_scores - log_norm[..., None]), 0.0)
        prob_grads = jnp.einsum(
            "rcgd,ncd->rcgn", gradient_heads, value_split, preferred_element_type=jnp.float32
        )
        score_grads = (probs * (prob_grads - out_dot[..., None]) * grad_scale).astype(jnp.bfloat16)
        weighted = (probs * gain_wide).astype(jnp.bfloat16)
        query_term = jnp.einsum(
            "rcgn,ncd->rcgd", score_grads, key_split, preferred_element_type=jnp.float32
        )
        key_term = jnp.einsum(
            "rcgn,rcgd->ncd", score_grads, heads_of_queries, preferred_element_type=jnp.float32
        )
        value_term = jnp.einsum(
            "rcgn,rcgd->ncd", weighted, gradient_heads, preferred_element_type=jnp.float32
        )
        length = key_block.shape[0]
        return (
            query_term,
            jnp.concatenate([key_term.reshape(length, -1), value_term.reshape(length, -1)], axis=1),
        )

    def grads_over(log_norm, query_start, key_portion, value_portion, offset):
        length = key_portion.shape[0]
        block_len, block_count = block_split(length)
        key_pos = lax.dynamic_slice_in_dim(all_positions, offset, length)

        def one_block(query_sum, inputs):
            query_term, pair_term = grads_block(log_norm, inputs[0], inputs[1], inputs[2])
            return (query_sum + query_term, pair_term)

        query_sum, pair_terms = lax.scan(
            one_block,
            query_start,
            (
                key_portion.reshape(block_count, block_len, -1),
                value_portion.reshape(block_count, block_len, -1),
                key_pos.reshape(block_count, block_len),
            ),
        )
        return (query_sum, pair_terms.reshape(length, -1))

    stats_start = (
        jnp.full((row_count, kv_local, group_width), very_low, jnp.float32),
        jnp.zeros((row_count, kv_local, group_width), jnp.float32),
    )
    query_zero = jnp.zeros((row_count, kv_local, group_width, HEAD_WIDTH), jnp.float32)
    pair_zero = jnp.zeros((row_count, 2 * kv_local * HEAD_WIDTH), jnp.float32)
    running = stats_start
    portion = lax.all_gather(key_loc, "ctx", axis=0, tiled=True)
    length = portion.shape[0]
    block_len, block_count = block_split(length)
    key_pos = all_positions
    running, unused = lax.scan(
        stats_block,
        running,
        (portion.reshape(block_count, block_len, -1), key_pos.reshape(block_count, block_len)),
    )
    running_max, denominator = running
    log_norm = running_max + jnp.log(denominator)

    def cycle_step(step, carry):
        key_block, value_block, pair_acc, query_sum = carry
        anchor = (my_index - step + cycle_count) % cycle_count
        offset = anchor * row_count
        query_sum, pair_terms = grads_over(log_norm, query_sum, key_block, value_block, offset)
        key_block, value_block = shifted((key_block, value_block), "ctx", 1)
        pair_acc = shifted(pair_acc + pair_terms, "ctx", 1)
        return (key_block, value_block, pair_acc, query_sum)

    unused_keys, unused_values, pair_share, query_sum = lax.fori_loop(
        0, cycle_count, cycle_step, (key_loc, value_loc, pair_zero, query_zero)
    )
    key_width = kv_local * HEAD_WIDTH
    query_part = query_sum.reshape(row_count, -1).astype(jnp.bfloat16)
    key_part = pair_share[:, :key_width].astype(jnp.bfloat16)
    value_part = pair_share[:, key_width:].astype(jnp.bfloat16)
    return (
        lax.all_to_all(query_part, "head", split_axis=0, concat_axis=1, tiled=True),
        lax.all_to_all(key_part, "head", split_axis=0, concat_axis=1, tiled=True),
        lax.all_to_all(value_part, "head", split_axis=0, concat_axis=1, tiled=True),
    )


def solution(mesh):
    in_specs = (
        P(("ctx", "head"), None),
        P(("ctx", "head"), None),
        P(("ctx", "head"), None),
        P(("ctx", "head"), None),
        P(("ctx", "head"), None),
        P("ctx"),
        P(),
    )
    out_specs = (P(("ctx", "head"), None), P(("ctx", "head"), None), P(("ctx", "head"), None))
    return jax.shard_map(
        on_device, mesh=mesh, in_specs=in_specs, out_specs=out_specs, check_vma=False
    )
```

profile of v0, /device:TPU:1, one launch (start us, length us, event | category | flops | bytes accessed | tf_op | source)
XLA Modules:
  0.0 1430.9 jit_solution(9999002778378512729)
XLA Ops:
  7.9 19.0 %all_to_all.137 = bf16[16,8,128]{2,0,1:T(8,128)(2,1)} all-to-all(bf16[16,8,128]{2,0,1:T(8,128)(2,1)S(1)} %copy_bitcast_fusion.6), channel_id=1, replica_groups=mesh['ctx'=64,'head'=8] {'head'}, dimensions={1} | all-to-all | bytes 65536 | tf_op jit(solution)/shard_map/all_to_all | solution.py:38
  40.6 5.0 all-to-all-start.3
  47.2 7.1 all-to-all-done.3
  60.3 7.5 all-to-all-done.4
  72.5 207.1 %all-gather.2.cloned.1.call-done = bf16[8192,128]{1,0:T(8,128)(2,1)} async-done(((bf16[128,128]{1,0:T(8,128)(2,1)}), bf16[8192,128]{1,0:T(8,128)(2,1)}) %all-gather.2.cloned.1.call-update) | async-done | bytes 2097168 | tf_op jit(solution)/shard_map/all_gather | solution.py:130
  279.6 26.5 %while.46 = (s32[]{:T(128)}, f32[128,1,4]{0,2,1:T(4,128)S(1)}, f32[128,1,4]{0,2,1:T(4,128)S(1)}, s32[16,512]{1,0:T(8,128)S(1)}, s32[128]{0:T(128)S(1)}, /*index=...) while((s32[]{:T(128)}, f32[128,1,4]{0,2,1:T(4,128)S(1)}, ...), condition=%wide.region_4.5_spmd.clone, body=%wide.region_1.4_spmd.clone.sunk | while | flops 68749824 | bytes 2589804 | solution.py:134
  306.1 964.0 %while.47 = (s32[]{:T(128)}, bf16[128,128]{1,0:T(8,128)(2,1)S(1)}, bf16[128,128]{1,0:T(8,128)(2,1)S(1)}, f32[128,256]{0,1:T(8,128)S(1)}, f32[128,1,4,128]{3,0,2,...) while((s32[]{:T(128)}, bf16[128,128]{1,0:T(8,128)(2,1)S(1)}, ...), condition=%wide.region_7.8_spmd.clone, body=%wide.region_6.7_spmd.clone.sunk | while | flops 84688912 | bytes 3808750 | solution.py:151
  317.1 4.5 collective-permute-done.2
  392.5 4.6 collective-permute-done.2
  511.5 4.7 collective-permute-done.2
  526.9 5.3 collective-permute-done.2
  588.2 4.5 collective-permute-done.2
  737.3 4.7 collective-permute-done.2
  752.7 5.3 collective-permute-done.2
  814.0 4.5 collective-permute-done.2
  963.1 4.7 collective-permute-done.2
  978.5 5.3 collective-permute-done.2
  1039.8 4.5 collective-permute-done.2
  1188.8 4.7 collective-permute-done.2
  1204.3 5.3 collective-permute-done.2
  1265.6 4.5 collective-permute-done.2
  1270.8 129.4 %all_to_all.138 = bf16[8,16,128]{2,1,0:T(8,128)(2,1)S(1)} all-to-all(bf16[8,16,128]{2,1,0:T(8,128)(2,1)S(1)} %bitcast.229), channel_id=1, replica_groups=mesh['ctx'=64,'head'=8] {'head'}, dimensions={0} | all-to-all | bytes 65536 | tf_op jit(solution)/shard_map/all_to_all | solution.py:161
  1405.1 6.3 all-to-all-done.6
  1416.6 6.8 all-to-all-done.5
  (1171 shorter events, 953.1 us)
Async XLA Ops:
  7.2 272.4 %all-gather.2.cloned.1.call-start = ((), (), s32[]{:S(2)}) async-start(), calls=%async_computation.8 | async-start | bytes 2129920 | tf_op jit(solution)/shard_map/all_gather | solution.py:130
  28.5 12.1 all-to-all-start.2
  40.6 13.7 all-to-all-start.3
  54.3 13.5 all-to-all-start.4
  67.8 238.3 %all-to-all-start.1 = ((bf16[16,8,128]{2,0,1:T(8,128)(2,1)}), bf16[16,8,128]{2,0,1:T(8,128)(2,1)S(1)}, u32[]{:S(2)}, u32[]{:S(2)}) async-start(bf16[16,8,128]{2,0,1:T(8,128)(2,1)} %copy_bitcast_fusion.5), calls=%async_computation.1 | async-start | bytes 65536 | tf_op jit(solution)/shard_map/all_to_all | solution.py:39
  356.1 10.4 collective-permute-start.2
  386.5 10.5 collective-permute-start.2
  505.5 10.6 collective-permute-start.2
  521.0 11.2 collective-permute-start.2
  537.1 10.4 collective-permute-start.2
  582.2 10.5 collective-permute-start.2
  731.3 10.6 collective-permute-start.2
  746.8 11.2 collective-permute-start.2
  762.9 10.4 collective-permute-start.2
  808.0 10.5 collective-permute-start.2
  957.1 10.6 collective-permute-start.2
  972.6 11.2 collective-permute-start.2
  988.7 10.4 collective-permute-start.2
  1033.8 10.5 collective-permute-start.2
  1182.9 10.6 collective-permute-start.2
  1198.4 11.2 collective-permute-start.2
  1259.6 10.5 collective-permute-start.2
  1400.2 11.2 all-to-all-start.6
  1411.4 12.0 all-to-all-start.5
  (178 other events, 1696.0 us)
Sparse Core Ops, SparseCore 0:
  27.1 252.4 all-gather.1
where the time goes:
time: 1440 us; the launch traced here: 1430 us
  waiting for transfers between devices  750 us (52%)
  starting transfers between devices  394 us (27%)
  blocking collectives  148 us (10%)
  matrix products  83.2 us (6%)
  other arithmetic  16.6 us (1%)
  local copies, waits for them, and re-layouts  15.7 us (1%)
    ppermute x192, waiting for transfers between devices, shifted(): lax.ppermute(array, axis, [(i, (i + by) % size) for i in range(size)])  512 us
    ppermute x192, starting transfers between devices, shifted(): lax.ppermute(array, axis, [(i, (i + by) % size) for i in range(size)])  369 us
    all_gather x1, waiting for transfers between devices, on_device(): portion = lax.all_gather(key_loc, 'ctx', axis=0, tiled=True)  207 us
    all_to_all x1, blocking collectives, on_device(): lax.all_to_all(value_part, 'head', split_axis=0, concat_axis=1, tiled=True)  129 us
    dot_general x80, matrix products, scores_of(): jnp.einsum('rcgd,ncd->rcgn', heads_of_queries, key_split, preferred_eleme...  31.8 us
  transfers between devices with their start and end apart: 199, of which 198 were waited for; matrix products, arithmetic and copies ran while one was open for 8% of the time, Pallas kernels for 0%

commit v1 on v0

--- a/solution.py
+++ b/solution.py
@@ -3,12 +3,19 @@
 import jax.numpy as jnp
 from jax import lax
 from jax.sharding import PartitionSpec as P
+from jax.lax import all_to_all, axis_size
 
 QUERY_HEADS = 32
 KEY_VALUE_HEADS = 8
 HEAD_WIDTH = 128
 CH = 64
 very_low = -1e30
+track_the_links = lambda local_values, group_axis: jnp.concatenate(
+    all_to_all(
+        jnp.stack([local_values] * axis_size(group_axis)), group_axis, split_axis=0, concat_axis=0
+    ),
+    axis=0,
+)
 
 
 def shifted(array, axis, by):
@@ -127,7 +134,7 @@
     query_zero = jnp.zeros((row_count, kv_local, group_width, HEAD_WIDTH), jnp.float32)
     pair_zero = jnp.zeros((row_count, 2 * kv_local * HEAD_WIDTH), jnp.float32)
     running = stats_start
-    portion = lax.all_gather(key_loc, "ctx", axis=0, tiled=True)
+    portion = track_the_links(key_loc, "ctx")
     length = portion.shape[0]
     block_len, block_count = block_split(length)
     key_pos = all_positions

time: 1440 us -> 1230 us (0.85)
  waiting for transfers between devices: 750 us -> 587 us
  blocking collectives: 148 us -> 93.7 us
  starting transfers between devices: 394 us -> 419 us
    all_gather x1 -> x0, waiting for transfers between devices: 207 us -> none  [on_device(): portion = lax.all_gather(key_loc, 'ctx', axis=0, tiled=True)]
    all_to_all x1, blocking collectives: 129 us -> 81.9 us  [on_device(): lax.all_to_all(value_part, 'head', split_axis=0, concat_axis=1, tiled=True)]
    all_to_all x1 -> x2, waiting for transfers between devices: 7.53 us -> 48.2 us  [the longest x1 42.5 us: all_to_all(jnp.stack([local_values] * axis_size(group_axis)), group_axis,...]
    all_to_all x1 -> x2, starting transfers between devices: 4.36 us -> 23 us  [the longest x1 11.8 us: on_device(): lax.all_to_all(keys, 'head', split_axis=1, concat_axis=0, tiled=True)]
  transfers between devices with their start and end apart: 199 -> 199, of which waited for: 198 -> 197; matrix products, arithmetic and copies ran while one was open for 8% -> 9% of each run, Pallas kernels for 0% -> 0%
where the time goes in v1:
time: 1230 us
  waiting for transfers between devices  587 us (48%)
  starting transfers between devices  419 us (34%)
  blocking collectives  93.7 us (8%)
  matrix products  83.1 us (7%)
  local copies, waits for them, and re-layouts  17.6 us (1%)
  other arithmetic  15.3 us (1%)
    ppermute x192, waiting for transfers between devices, shifted(): lax.ppermute(array, axis, [(i, (i + by) % size) for i in range(size)])  512 us
    ppermute x192, starting transfers between devices, shifted(): lax.ppermute(array, axis, [(i, (i + by) % size) for i in range(size)])  371 us
    all_to_all x1, blocking collectives, on_device(): lax.all_to_all(value_part, 'head', split_axis=0, concat_axis=1, tiled=True)  81.9 us
    all_to_all x1, waiting for transfers between devices, all_to_all(jnp.stack([local_values] * axis_size(group_axis)), group_axis,...  42.5 us
    dot_general x80, matrix products, scores_of(): jnp.einsum('rcgd,ncd->rcgn', heads_of_queries, key_split, preferred_eleme...  31.8 us
  transfers between devices with their start and end apart: 199, of which 197 were waited for; matrix products, arithmetic and copies ran while one was open for 9% of the time, Pallas kernels for 0%

profile of v1, /device:TPU:1, one launch (start us, length us, event | category | flops | bytes accessed | tf_op | source)
XLA Modules:
  0.0 1225.1 jit_solution(5955161773192698058)
XLA Ops:
  2.0 11.8 all-to-all-start
  15.4 5.7 all-to-all-done
  26.7 6.5 all-to-all-done.2
  33.2 5.0 all-to-all-start.4
  39.1 7.3 all-to-all-done.4
  46.4 11.8 all_to_all.142
  60.1 11.2 all-to-all-start.3
  75.4 42.5 %all-to-all-done.3 = bf16[64,128,128]{2,1,0:T(8,128)(2,1)} async-done(((bf16[64,128,128]{2,1,0:T(8,128)(2,1)}), bf16[64,128,128]{2,1,0:T(8,128)(2,1)}, u32[]{:S(2)}, u32[]{:S(2)}) %all-to-all-start.3) | async-done | bytes 2097184 | tf_op jit(solution)/shard_map/all_to_all | solution.py:14
  117.9 8.4 all-to-all-start.1
  126.3 26.5 %while.46 = (s32[]{:T(128)}, f32[128,1,4]{0,2,1:T(4,128)S(1)}, f32[128,1,4]{0,2,1:T(4,128)S(1)}, s32[16,512]{1,0:T(8,128)S(1)}, s32[128]{0:T(128)S(1)}, /*index=...) while((s32[]{:T(128)}, f32[128,1,4]{0,2,1:T(4,128)S(1)}, ...), condition=%wide.region_4.5_spmd.clone, body=%wide.region_1.4_spmd.clone.sunk | while | flops 68749824 | bytes 2589804 | solution.py:141
  152.8 965.8 %while.47 = (s32[]{:T(128)}, bf16[128,128]{1,0:T(8,128)(2,1)S(1)}, bf16[128,128]{1,0:T(8,128)(2,1)S(1)}, f32[128,256]{0,1:T(8,128)S(1)}, f32[128,1,4,128]{3,0,2,...) while((s32[]{:T(128)}, bf16[128,128]{1,0:T(8,128)(2,1)S(1)}, ...), condition=%wide.region_7.8_spmd.clone, body=%wide.region_6.7_spmd.clone.sunk | while | flops 84688912 | bytes 3808750 | solution.py:158
  164.7 5.6 collective-permute-done.2
  211.1 4.6 collective-permute-done.2
  360.0 4.7 collective-permute-done.2
  375.5 5.3 collective-permute-done.2
  585.8 4.7 collective-permute-done.2
  601.3 5.3 collective-permute-done.2
  811.6 4.7 collective-permute-done.2
  827.1 5.3 collective-permute-done.2
  1037.4 4.7 collective-permute-done.2
  1052.9 5.3 collective-permute-done.2
  1119.4 81.9 %all_to_all.143 = bf16[8,16,128]{2,1,0:T(8,128)(2,1)S(1)} all-to-all(bf16[8,16,128]{2,1,0:T(8,128)(2,1)S(1)} %bitcast.229), channel_id=1, replica_groups=mesh['ctx'=64,'head'=8] {'head'}, dimensions={0} | all-to-all | bytes 65536 | tf_op jit(solution)/shard_map/all_to_all | solution.py:168
  1206.1 6.3 all-to-all-done.7
  1217.6 6.8 all-to-all-done.6
  (1173 shorter events, 960.6 us)
Async XLA Ops:
  2.0 19.1 %all-to-all-start = ((bf16[16,8,128]{2,0,1:T(8,128)(2,1)}), bf16[16,8,128]{2,0,1:T(8,128)(2,1)S(1)}, u32[]{:S(2)}, u32[]{:S(2)}) async-start(bf16[16,8,128]{2,0,1:T(8,128)(2,1)} %copy_bitcast_fusion.6), calls=%async_computation | async-start | bytes 65536 | tf_op jit(solution)/shard_map/all_to_all | solution.py:45
  21.1 12.1 all-to-all-start.2
  33.2 13.2 %all-to-all-start.4 = ((bf16[16,8,512]{2,0,1:T(8,128)(2,1)}), bf16[16,8,512]{2,0,1:T(8,128)(2,1)S(1)}, u32[]{:S(2)}, u32[]{:S(2)}) async-start(bf16[16,8,512]{2,0,1:T(8,128)(2,1)} %bitcast.157), calls=%async_computation.4 | async-start | bytes 262144 | tf_op jit(solution)/shard_map/all_to_all | solution.py:44
  60.1 57.8 %all-to-all-start.3 = ((bf16[64,128,128]{2,1,0:T(8,128)(2,1)}), bf16[64,128,128]{2,1,0:T(8,128)(2,1)}, u32[]{:S(2)}, u32[]{:S(2)}) async-start(bf16[64,128,128]{2,1,0:T(8,128)(2,1)} %stack.2), calls=%async_computation.3 | async-start | bytes 4194304 | tf_op jit(solution)/shard_map/all_to_all | solution.py:14
  117.9 34.9 %all-to-all-start.1 = ((bf16[16,8,128]{2,0,1:T(8,128)(2,1)}), bf16[16,8,128]{2,0,1:T(8,128)(2,1)S(1)}, u32[]{:S(2)}, u32[]{:S(2)}) async-start(bf16[16,8,128]{2,0,1:T(8,128)(2,1)} %copy_bitcast_fusion.5), calls=%async_computation.1 | async-start | bytes 65536 | tf_op jit(solution)/shard_map/all_to_all | solution.py:46
  159.9 10.5 collective-permute-start.2
  205.2 10.5 collective-permute-start.2
  354.1 10.6 collective-permute-start.2
  369.6 11.2 collective-permute-start.2
  385.7 10.4 collective-permute-start.2
  430.8 10.5 collective-permute-start.2
  579.9 10.6 collective-permute-start.2
  595.4 11.2 collective-permute-start.2
  611.4 10.3 collective-permute-start.2
  656.6 10.5 collective-permute-start.2
  805.7 10.6 collective-permute-start.2
  821.1 11.2 collective-permute-start.2
  837.2 10.4 collective-permute-start.2
  882.4 10.5 collective-permute-start.2
  1031.5 10.6 collective-permute-start.2
  1046.9 11.2 collective-permute-start.2
  1108.2 10.5 collective-permute-start.2
  1201.3 11.1 all-to-all-start.7
  1212.4 12.0 all-to-all-start.6
  (179 other events, 1658.0 us)
